TPU v7x, 256 devices: a whole 4x4x8 slice. The times are simulated.
256 devices in a mesh: row: 16 (over y, z_lo, core), col: 16 (over z_hi, x).
Axes of the slice: x: 4, y: 4, z: 8 (z_hi: 4, z_lo: 2; z = z_hi * 2 + z_lo), core: 2. Of those that a mesh axis runs over, the one named last changes fastest.
Arguments:
- tokens: bfloat16 [4096, 8192], P('col', 'row'), may hold values from -6 to 6
- grad_out: bfloat16 [4096, 16384], P('row', 'col'), may hold values from -6 to 6
- base_weight: float32 [8192, 16384], P('row', 'col'), may hold values from -6 to 6
- left_param: float32 [16, 512, 512], P('row'), may hold values from -6 to 6
- right_param: float32 [64, 256, 256], P('col'), may hold values from -6 to 6
Outputs:
- rotated_weight: float32 [8192, 16384], P('row', 'col')
- new_left: float32 [16, 512, 512], P('row')
- new_right: float32 [64, 256, 256], P('col')
All inputs are finite; a program needn't handle non-finite values.
Results may differ from a plain program's by a relative error of at most 0.0003.
Values may be sent and summed in bfloat16 or wider, within the bound.
A program may use at most 128 MiB of HBM per device.

v0:
```python
import math
import jax
import jax.numpy as jnp
from jax import lax
from jax.sharding import PartitionSpec as P

precise = lax.Precision.HIGHEST
taylor_degree = 6
step_rate = 0.3
epsilon = 1e-06


def batch_product(first, second):
    return jnp.einsum("lab,lbc->lac", first, second, precision=precise)


def transpose_last(matrix):
    return jnp.swapaxes(matrix, 1, 2)


def skew_from(param):
    skew_scale = 0.5 / math.sqrt(param.shape[-1])
    return skew_scale * (param - transpose_last(param))


def column_levels(skew, col_start, col_width):
    dimension = skew.shape[-1]
    eye_part = (
        jnp.arange(dimension)[:, None] == col_start + jnp.arange(col_width)[None, :]
    ).astype(jnp.float32)
    current = (
        eye_part[None] + lax.dynamic_slice_in_dim(skew, col_start, col_width, 2) / taylor_degree
    )
    horner_levels = [current] * (taylor_degree + 1)
    for divisor in range(taylor_degree - 1, 0, -1):
        current = eye_part[None] + batch_product(skew, current) / divisor
        horner_levels[divisor] = current
    return horner_levels


def adjoint(skew, horner_levels, upper_grad):
    running = jnp.zeros(skew.shape, jnp.float32)
    for divisor in range(1, taylor_degree):
        running = (
            running
            + batch_product(upper_grad, transpose_last(horner_levels[divisor + 1])) / divisor
        )
        upper_grad = batch_product(transpose_last(skew), upper_grad) / divisor
    return (running, upper_grad)


def update_param(param, accum):
    skew_scale = 0.5 / math.sqrt(param.shape[-1])
    grad_param = skew_scale * (accum - transpose_last(accum))
    root_mean = jnp.sqrt(jnp.mean(grad_param * grad_param, axis=(1, 2), keepdims=True) + epsilon)
    return param - step_rate * grad_param / root_mean


def right_apply(weight, rotation):
    count = rotation.shape[0]
    block = rotation.shape[-1]
    shaped = weight.reshape(weight.shape[0], count, block)
    return jnp.einsum("nbr,brs->nbs", shaped, rotation, precision=precise).reshape(weight.shape)


def body(tokens, grad_out, base_weight, left_param, right_param):
    col_count = lax.axis_size("col")
    left_size = left_param.shape[-1]
    left_count = left_param.shape[0]
    right_size = right_param.shape[-1]
    right_count = right_param.shape[0]
    row_total = base_weight.shape[0]
    col_total = base_weight.shape[1]
    col_width = left_size // col_count
    col_start = lax.axis_index("col") * col_width
    left_skew = skew_from(left_param)
    right_skew = skew_from(right_param)
    left_cols = column_levels(left_skew, col_start, col_width)
    right_levels = column_levels(right_skew, 0, right_size)
    right_rot = right_levels[1]
    token_all = lax.all_gather(tokens, "col", axis=0, tiled=True)
    left_rot = lax.all_gather(left_cols[1], "col", axis=2, tiled=True)
    grads_all = lax.all_gather(grad_out, "row", axis=0, tiled=True)
    grad_weight = lax.dot_general(
        token_all, grads_all, (((0,), (0,)), ((), ())), preferred_element_type=jnp.float32
    )
    weight_blocks = base_weight.reshape(left_count, left_size, col_total)
    grad_blocks = grad_weight.reshape(left_count, left_size, col_total)
    mixed_weight = right_apply(base_weight, right_rot).reshape(left_count, left_size, col_total)
    left_part = jnp.einsum("lnc,lmc->lnm", grad_blocks, mixed_weight, precision=precise)
    rotated = batch_product(left_rot, weight_blocks).reshape(row_total, right_count, right_size)
    right_part = jnp.einsum(
        "nbr,nbs->brs",
        rotated,
        grad_weight.reshape(row_total, right_count, right_size),
        precision=precise,
    )
    right_grad = lax.psum(right_part, "row")
    upper_piece = lax.psum_scatter(left_part, "col", scatter_dimension=2, tiled=True)
    partial_sum, upper_piece = adjoint(left_skew, left_cols, upper_piece)
    placed = lax.dynamic_update_slice_in_dim(
        jnp.zeros_like(partial_sum), upper_piece / taylor_degree, col_start, 2
    )
    left_acc = lax.psum(partial_sum + placed, "col")
    right_acc, right_upper = adjoint(right_skew, right_levels, right_grad)
    right_acc = right_acc + right_upper / taylor_degree
    new_left = update_param(left_param, left_acc)
    new_right = update_param(right_param, right_acc)
    new_left_skew = skew_from(new_left)
    new_cols = column_levels(new_left_skew, col_start, col_width)[1]
    new_left_rot = lax.all_gather(new_cols, "col", axis=2, tiled=True)
    new_right_rot = column_levels(skew_from(new_right), 0, right_size)[1]
    turned = batch_product(new_left_rot, weight_blocks).reshape(row_total, col_total)
    rotated_weight = right_apply(turned, new_right_rot)
    return (rotated_weight, new_left, new_right)


def solution(mesh):
    return jax.shard_map(
        body,
        mesh=mesh,
        in_specs=(
            P("col", "row"),
            P("row", "col"),
            P("row", "col"),
            P("row", None, None),
            P("col", None, None),
        ),
        out_specs=(P("row", "col"), P("row", None, None), P("col", None, None)),
        check_vma=False,
    )
```

profile of v0, /device:TPU:8, one launch (start us, length us, event | category | flops | bytes accessed | tf_op | source)
XLA Modules:
  0.0 776.7 jit_solution(18041137845352495483)
XLA Ops:
  19.4 1.9 fusion.28
  21.3 1.9 fusion.27
  23.3 1.9 fusion.26
  31.0 5.0 fusion
  36.1 52.4 %all-gather.7.cloned.1.call-done = bf16[4096,512]{1,0:T(8,128)(2,1)} async-done(((bf16[256,512]{1,0:T(8,128)(2,1)}), bf16[4096,512]{1,0:T(8,128)(2,1)}) %all-gather.7.cloned.1.call-update) | async-done | bytes 4194320 | tf_op jit(solution)/shard_map/all_gather | solution.py:81
  88.4 56.7 %all-gather.9.cloned.1.call-done = bf16[4096,1024]{1,0:T(8,128)(2,1)} async-done(((bf16[256,1024]{1,0:T(8,128)(2,1)}), bf16[4096,1024]{1,0:T(8,128)(2,1)}) %all-gather.9.cloned.1.call-update) | async-done | bytes 8388624 | tf_op jit(solution)/shard_map/all_gather | solution.py:83
  145.1 8.3 %fusion.122 = f32[512,1024]{1,0:T(8,128)S(1)} fusion(bf16[4096,512]{1,0:T(8,128)(2,1)} %all-gather.7.cloned.1.call-done, bf16[4096,1024]{1,0:T(8,128)(2,1)} %all-gather.9.cloned.1.call-done), kind=kOutput, calls=%fused_computation.176 | convolution fusion | flops 4294967296 | bytes 14680064 | tf_op jit(solution)/shard_map/dot_general | solution.py:84
  154.8 4.5 convolution_bitcast_fusion
  159.3 3.6 copy.45
  162.9 39.3 %all-gather.11.cloned.1.call-done = f32[512,512]{0,1:T(8,128)} async-done(((f32[512,32]{0,1:T(8,128)}), f32[512,512]{0,1:T(8,128)}) %all-gather.11.cloned.1.call-update) | async-done | bytes 1048592 | tf_op jit(solution)/shard_map/all_gather | solution.py:82
  202.2 5.5 fusion.7
  207.8 3.1 fusion.2
  212.6 158.8 %all-reduce.9.cloned.1.call-done = f32[1,512,512]{1,0,2:T(1,128)} async-done(((f32[1,512,512]{1,0,2:T(1,128)}), f32[1,512,512]{1,0,2:T(1,128)}) %all-reduce.9.cloned.1.call-update) | async-done | bytes 1048592
  373.9 2.8 fusion.84
  376.7 116.3 %all-reduce.5.cloned.1.call-done = f32[4,256,256]{2,1,0:T(8,128)} async-done(((f32[4,256,256]{2,1,0:T(8,128)}), f32[4,256,256]{2,1,0:T(8,128)}) %all-reduce.5.cloned.1.call-update) | async-done | bytes 1048592 | tf_op jit(solution)/shard_map/psum | solution.py:98
  493.0 2.4 fusion.78
  497.8 2.1 convolution_multiply_fusion.10
  503.7 2.2 fusion.22
  516.4 3.0 fusion.21
  519.3 2.2 fusion.20
  525.9 165.5 %all-reduce.7.cloned.1.call-done = f32[1,512,512]{1,2,0:T(8,128)} async-done(((f32[1,512,512]{1,2,0:T(8,128)}), f32[1,512,512]{1,2,0:T(8,128)}) %all-reduce.7.cloned.1.call-update) | async-done | bytes 1048592 | tf_op jit(solution)/shard_map/psum | solution.py:104
  691.4 2.6 copy.46
  694.1 3.0 multiply_reduce_fusion
  697.8 2.5 copy.47
  708.6 1.9 fusion.19
  710.6 2.1 fusion.18
  712.7 1.9 fusion.17
  714.7 1.9 fusion.16
  716.6 2.9 convolution_add_fusion.1
  719.5 40.1 %all-gather.13.cloned.1.call-done = f32[512,512]{0,1:T(8,128)} async-done(((f32[512,32]{0,1:T(8,128)}), f32[512,512]{0,1:T(8,128)}) %all-gather.13.cloned.1.call-update) | async-done | bytes 1048592 | tf_op jit(solution)/shard_map/all_gather | solution.py:111
  759.6 4.7 fusion.5
  764.4 3.5 fusion.124
  (123 shorter events, 53.6 us)
Async XLA Ops:
  7.2 3.1 copy-start.2
  7.2 81.3 %all-gather.7.cloned.1.call-start = ((), (), s32[]{:S(2)}) async-start(), calls=%async_computation | async-start | bytes 4456448 | tf_op jit(solution)/shard_map/all_gather | solution.py:81
  7.9 137.2 %all-gather.9.cloned.1.call-start = ((), (), s32[]{:S(2)}) async-start(), calls=%async_computation.1 | async-start | bytes 8912896 | tf_op jit(solution)/shard_map/all_gather | solution.py:83
  8.7 193.5 %all-gather.11.cloned.1.call-start = ((), (), s32[]{:S(2)}) async-start(), calls=%async_computation.4 | async-start | bytes 1114112 | tf_op jit(solution)/shard_map/all_gather | solution.py:82
  12.0 4.3 copy-start.3
  12.8 2.1 copy-start.26
  13.5 1.4 copy-start.28
  14.9 356.4 %all-reduce.9.cloned.1.call-start = ((), (), s32[]{:S(2)}) async-start(), calls=%async_computation.6 | async-start | bytes 2097152
  17.6 1.7 copy-start.20
  21.3 1.9 copy-start.10
  23.3 1.9 copy-start.12
  29.1 1.9 copy-start
  145.1 9.7 %copy-start.19 = (f32[4,256,512]{2,1,0:T(8,128)S(1)}, f32[4,256,512]{2,1,0:T(8,128)}, u32[]{:S(2)}) copy-start(f32[4,256,512]{2,1,0:T(8,128)} %fusion) | copy-start | bytes 6291460
  153.5 1.3 copy-start.17
  162.9 330.1 %all-reduce.5.cloned.1.call-start = ((), (), s32[]{:S(2)}) async-start(), calls=%async_computation.2 | async-start | bytes 2097152 | tf_op jit(solution)/shard_map/psum | solution.py:98
  202.2 5.6 copy-start.18
  207.7 3.6 copy-start.30
  210.9 480.6 %all-reduce.7.cloned.1.call-start = ((), (), s32[]{:S(2)}) async-start(), calls=%async_computation.3 | async-start | bytes 2097152 | tf_op jit(solution)/shard_map/psum | solution.py:104
  497.8 2.2 copy-start.6
  497.8 2.2 copy-start.22
  500.0 1.2 copy-start.15
  502.4 1.2 copy-start.11
  503.6 2.2 copy-start.29
  505.8 3.4 copy-start.24
  505.8 3.4 copy-start.27
  516.3 3.0 copy-start.8
  516.3 243.3 %all-gather.13.cloned.1.call-start = ((), (), s32[]{:S(2)}) async-start(), calls=%async_computation.5 | async-start | bytes 1114112 | tf_op jit(solution)/shard_map/all_gather | solution.py:111
  521.5 1.7 copy-start.16
  691.4 2.6 copy-start.25
  704.2 2.9 copy-start.4
  716.6 43.0 %copy-start.1 = (f32[512,1024]{1,0:T(8,128)S(1)}, f32[512,1024]{1,0:T(8,128)}, u32[]{:S(2)}) copy-start(f32[512,1024]{1,0:T(8,128)} %param.7) | copy-start | bytes 6291460
  719.5 44.9 %copy-start.23 = (f32[4,256,256]{2,1,0:T(8,128)S(1)}, f32[4,256,256]{2,1,0:T(8,128)}, u32[]{:S(2)}) copy-start(f32[4,256,256]{2,1,0:T(8,128)} %convolution_add_fusion.1) | copy-start | bytes 3145732
  (6 other events, 6.1 us)
Sparse Core Ops, SparseCore 0:
  10.4 77.9 all-gather.6
  90.3 54.8 all-gather.8
  147.6 54.5 all-gather.10
  204.7 166.6 all-reduce.8
  374.4 118.5 all-reduce.4
  516.4 174.9 all-reduce.6
  707.2 52.3 all-gather.12
where the time goes:
time: 781 us; the launch traced here: 777 us
  waiting for transfers between devices  631 us (81%)
  matrix products  95.4 us (12%)
  local copies, waits for them, and re-layouts  25.2 us (3%)
  between operations  16.4 us (2%)
  other arithmetic  8.11 us (1%)
    psum x1, waiting for transfers between devices, body(): left_acc = lax.psum(partial_sum + placed, 'col')  166 us
    unnamed x8, waiting for transfers between devices  160 us
    psum x1, waiting for transfers between devices, body(): right_grad = lax.psum(right_part, 'row')  116 us
    dot_general x42, matrix products, batch_product(): return jnp.einsum('lab,lbc->lac', first, second, precision=precise)  71 us
    all_gather x1, waiting for transfers between devices, body(): grads_all = lax.all_gather(grad_out, 'row', axis=0, tiled=True)  56.7 us
    all_gather x1, waiting for transfers between devices, body(): token_all = lax.all_gather(tokens, 'col', axis=0, tiled=True)  52.4 us
    all_gather x1, waiting for transfers between devices, body(): new_left_rot = lax.all_gather(new_cols, 'col', axis=2, tiled=True)  40.1 us
    all_gather x1, waiting for transfers between devices, body(): left_rot = lax.all_gather(left_cols[1], 'col', axis=2, tiled=True)  39.3 us
  transfers between devices with their start and end apart: 7, of which 7 were waited for; matrix products, arithmetic and copies ran while one was open for 10% of the time, Pallas kernels for 0%

commit v1 on v0

--- a/solution.py
+++ b/solution.py
@@ -79,7 +79,9 @@
     right_levels = column_levels(right_skew, 0, right_size)
     right_rot = right_levels[1]
     token_all = lax.all_gather(tokens, "col", axis=0, tiled=True)
-    left_rot = lax.all_gather(left_cols[1], "col", axis=2, tiled=True)
+    left_rot = jnp.concatenate(
+        lax.all_to_all(jnp.stack([left_cols[1]] * lax.axis_size("col")), "col", 0, 0), axis=2
+    )
     grads_all = lax.all_gather(grad_out, "row", axis=0, tiled=True)
     grad_weight = lax.dot_general(
         token_all, grads_all, (((0,), (0,)), ((), ())), preferred_element_type=jnp.float32

time: 781 us -> 745 us (0.954)
  waiting for transfers between devices: 631 us -> 584 us
  starting transfers between devices: 1.15 us -> 12.4 us
    all_gather x1 -> x0, waiting for transfers between devices: 39.3 us -> none  [body(): left_rot = lax.all_gather(left_cols[1], 'col', axis=2, tiled=True)]
    all_to_all x0 -> x1, starting transfers between devices: none -> 11.1 us  [body(): lax.all_to_all(jnp.stack([left_cols[1]] * lax.axis_size('col')), 'col', 0...]
    psum x1, waiting for transfers between devices: 116 us -> 107 us  [body(): right_grad = lax.psum(right_part, 'row')]
    all_gather x1, waiting for transfers between devices: 52.4 us -> 60.4 us  [body(): token_all = lax.all_gather(tokens, 'col', axis=0, tiled=True)]
    unnamed x8 -> x7, waiting for transfers between devices: 160 us -> 159 us
  transfers between devices with their start and end apart: 7 -> 7, of which waited for: 7 -> 6; matrix products, arithmetic and copies ran while one was open for 10% -> 13% of each run, Pallas kernels for 0% -> 0%
where the time goes in v1:
time: 745 us; the launch traced here: 740 us
  waiting for transfers between devices  584 us (78%)
  matrix products  91.9 us (12%)
  local copies, waits for them, and re-layouts  27.1 us (4%)
  between operations  16.4 us (2%)
  starting transfers between devices  12.4 us (2%)
  other arithmetic  8.48 us (1%)
    psum x1, waiting for transfers between devices, body(): left_acc = lax.psum(partial_sum + placed, 'col')  160 us
    unnamed x7, waiting for transfers between devices  159 us
    psum x1, waiting for transfers between devices, body(): right_grad = lax.psum(right_part, 'row')  107 us
    dot_general x42, matrix products, batch_product(): return jnp.einsum('lab,lbc->lac', first, second, precision=precise)  67.4 us
    all_gather x1, waiting for transfers between devices, body(): token_all = lax.all_gather(tokens, 'col', axis=0, tiled=True)  60.4 us
    all_gather x1, waiting for transfers between devices, body(): grads_all = lax.all_gather(grad_out, 'row', axis=0, tiled=True)  56.7 us
    all_gather x1, waiting for transfers between devices, body(): new_left_rot = lax.all_gather(new_cols, 'col', axis=2, tiled=True)  40.1 us
  transfers between devices with their start and end apart: 7, of which 6 were waited for; matrix products, arithmetic and copies ran while one was open for 13% of the time, Pallas kernels for 0%

profile of v1, /device:TPU:8, one launch (start us, length us, event | category | flops | bytes accessed | tf_op | source)
XLA Modules:
  0.0 740.2 jit_solution(9288583220795203699)
XLA Ops:
  15.3 11.1 %all-to-all-start = ((f32[16,1,512,32]{2,3,1,0:T(8,128)}), f32[16,1,512,32]{2,3,1,0:T(8,128)}, u32[]{:S(2)}, u32[]{:S(2)}) async-start(f32[16,1,512,32]{2,3,1,0:T(8,128)} %stack.2), calls=%async_computation | async-start | bytes 2097152 | tf_op jit(solution)/shard_map/all_to_all | solution.py:83
  30.8 1.9 fusion.22
  32.8 1.9 fusion.21
  34.8 1.9 fusion.20
  36.7 1.9 fusion.19
  39.6 1.9 convolution_add_fusion
  41.6 5.0 fusion
  46.6 60.4 %all-gather.5.cloned.1.call-done = bf16[4096,512]{1,0:T(8,128)(2,1)} async-done(((bf16[256,512]{1,0:T(8,128)(2,1)}), bf16[4096,512]{1,0:T(8,128)(2,1)}) %all-gather.5.cloned.1.call-update) | async-done | bytes 4194320 | tf_op jit(solution)/shard_map/all_gather | solution.py:81
  107.0 56.7 %all-gather.7.cloned.1.call-done = bf16[4096,1024]{1,0:T(8,128)(2,1)} async-done(((bf16[256,1024]{1,0:T(8,128)(2,1)}), bf16[4096,1024]{1,0:T(8,128)(2,1)}) %all-gather.7.cloned.1.call-update) | async-done | bytes 8388624 | tf_op jit(solution)/shard_map/all_gather | solution.py:85
  163.7 8.3 %fusion.117 = f32[512,1024]{1,0:T(8,128)S(1)} fusion(bf16[4096,512]{1,0:T(8,128)(2,1)} %all-gather.5.cloned.1.call-done, bf16[4096,1024]{1,0:T(8,128)(2,1)} %all-gather.7.cloned.1.call-done), kind=kOutput, calls=%fused_computation.171 | convolution fusion | flops 4294967296 | bytes 14680064 | tf_op jit(solution)/shard_map/dot_general | solution.py:86
  173.4 4.5 convolution_bitcast_fusion
  177.9 3.6 copy.78
  181.6 2.9 copy.103
  185.8 5.5 fusion.116
  191.3 3.1 fusion.3
  194.7 157.7 %all-reduce.9.cloned.1.call-done = f32[1,512,512]{1,0,2:T(1,128)} async-done(((f32[1,512,512]{1,0,2:T(1,128)}), f32[1,512,512]{1,0,2:T(1,128)}) %all-reduce.9.cloned.1.call-update) | async-done | bytes 1048592
  354.3 1.9 fusion.78
  366.9 107.2 %all-reduce.5.cloned.1.call-done = f32[4,256,256]{2,1,0:T(8,128)} async-done(((f32[4,256,256]{2,1,0:T(8,128)}), f32[4,256,256]{2,1,0:T(8,128)}) %all-reduce.5.cloned.1.call-update) | async-done | bytes 1048592 | tf_op jit(solution)/shard_map/psum | solution.py:100
  474.2 2.4 fusion.72
  491.3 160.4 %all-reduce.7.cloned.1.call-done = f32[1,512,512]{1,2,0:T(8,128)} async-done(((f32[1,512,512]{1,2,0:T(8,128)}), f32[1,512,512]{1,2,0:T(8,128)}) %all-reduce.7.cloned.1.call-update) | async-done | bytes 1048592 | tf_op jit(solution)/shard_map/psum | solution.py:106
  651.7 2.6 copy.79
  654.3 3.0 multiply_reduce_fusion
  658.0 2.5 copy.80
  668.9 1.9 fusion.13
  670.8 1.9 fusion.12
  672.7 1.9 fusion.11
  674.7 2.1 fusion.10
  676.8 2.9 convolution_add_fusion.1
  679.7 40.1 %all-gather.9.cloned.1.call-done = f32[512,512]{0,1:T(8,128)} async-done(((f32[512,32]{0,1:T(8,128)}), f32[512,512]{0,1:T(8,128)}) %all-gather.9.cloned.1.call-update) | async-done | bytes 1048592 | tf_op jit(solution)/shard_map/all_gather | solution.py:113
  719.9 7.9 %fusion.34 = f32[512,4,256]{2,0,1:T(8,128)S(1)} fusion(f32[4,256,512]{2,1,0:T(8,128)S(1)} %bitcast.150, f32[512,512]{0,1:T(8,128)} %all-gather.9.cloned.1.call-done), kind=kOutput, calls=%fused_computation.71 | convolution fusion | flops 3221225472 | bytes 5242880 | tf_op jit(solution)/shard_map/lab,lbc->lac/dot_general | solution.py:14
  727.8 3.5 fusion.119
  731.3 1.8 copy.84
  (118 shorter events, 51.1 us)
Async XLA Ops:
  7.2 3.1 copy-start.1
  7.2 99.9 %all-gather.5.cloned.1.call-start = ((), (), s32[]{:S(2)}) async-start(), calls=%async_computation.1 | async-start | bytes 4456448 | tf_op jit(solution)/shard_map/all_gather | solution.py:81
  7.9 155.8 %all-gather.7.cloned.1.call-start = ((), (), s32[]{:S(2)}) async-start(), calls=%async_computation.2 | async-start | bytes 8912896 | tf_op jit(solution)/shard_map/all_gather | solution.py:85
  12.7 2.6 copy-start.24
  13.5 1.9 copy-start.26
  14.2 13.6 %copy-start.2 = (f32[4,256,256]{2,1,0:T(8,128)S(1)}, f32[4,256,256]{2,1,0:T(8,128)}, u32[]{:S(2)}) copy-start(f32[4,256,256]{2,1,0:T(8,128)} %param.9) | copy-start | bytes 3145732
  15.3 170.4 %all-to-all-start = ((f32[16,1,512,32]{2,3,1,0:T(8,128)}), f32[16,1,512,32]{2,3,1,0:T(8,128)}, u32[]{:S(2)}, u32[]{:S(2)}) async-start(f32[16,1,512,32]{2,3,1,0:T(8,128)} %stack.2), calls=%async_computation | async-start | bytes 2097152 | tf_op jit(solution)/shard_map/all_to_all | solution.py:83
  26.4 326.0 %all-reduce.9.cloned.1.call-start = ((), (), s32[]{:S(2)}) async-start(), calls=%async_computation.6 | async-start | bytes 2097152
  29.1 1.7 copy-start.18
  32.8 1.9 copy-start.8
  34.8 3.9 copy-start.10
  36.7 4.9 copy-start.12
  38.6 1.0 copy-start.4
  39.6 1.9 copy-start.14
  163.7 9.7 %copy-start.17 = (f32[4,256,512]{2,1,0:T(8,128)S(1)}, f32[4,256,512]{2,1,0:T(8,128)}, u32[]{:S(2)}) copy-start(f32[4,256,512]{2,1,0:T(8,128)} %fusion) | copy-start | bytes 6291460
  172.1 1.3 copy-start.15
  181.5 292.6 %all-reduce.5.cloned.1.call-start = ((), (), s32[]{:S(2)}) async-start(), calls=%async_computation.3 | async-start | bytes 2097152 | tf_op jit(solution)/shard_map/psum | solution.py:100
  181.6 2.9 copy-start.27
  185.8 5.6 copy-start.16
  194.5 457.2 %all-reduce.7.cloned.1.call-start = ((), (), s32[]{:S(2)}) async-start(), calls=%async_computation.4 | async-start | bytes 2097152 | tf_op jit(solution)/shard_map/psum | solution.py:106
  353.2 5.1 copy-start.25
  366.5 353.4 %all-gather.9.cloned.1.call-start = ((), (), s32[]{:S(2)}) async-start(), calls=%async_computation.5 | async-start | bytes 1114112 | tf_op jit(solution)/shard_map/all_gather | solution.py:113
  476.6 1.2 copy-start.5
  476.6 1.5 copy-start.21
  478.1 1.2 copy-start.13
  480.6 1.2 copy-start.11
  483.0 1.2 copy-start.9
  484.2 1.2 copy-start.19
  651.7 2.6 copy-start.23
  664.5 2.9 copy-start.3
  676.8 43.0 %copy-start = (f32[1024,512]{1,0:T(8,128)S(1)}, f32[1024,512]{1,0:T(8,128)}, u32[]{:S(2)}) copy-start(f32[1024,512]{1,0:T(8,128)} %copy.103) | copy-start | bytes 6291460
  679.7 48.1 %copy-start.22 = (f32[4,256,256]{2,1,0:T(8,128)S(1)}, f32[4,256,256]{2,1,0:T(8,128)}, u32[]{:S(2)}) copy-start(f32[4,256,256]{2,1,0:T(8,128)} %convolution_add_fusion.1) | copy-start | bytes 3145732
  (3 other events, 2.9 us)
Sparse Core Ops, SparseCore 0:
  10.4 96.5 all-gather.4
  108.9 54.8 all-gather.6
  181.7 170.6 all-reduce.8
  355.5 118.6 all-reduce.4
  476.7 174.9 all-reduce.6
  667.4 52.3 all-gather.8
